TPU v7x, 128 devices: a whole 4x4x4 slice. The times are simulated.
128 devices in a mesh: obs: 4 (over x_hi, core), state: 32 (over y, x_lo, z).
Axes of the slice: x: 4 (x_hi: 2, x_lo: 2; x = x_hi * 2 + x_lo), y: 4, z: 4, core: 2. Of those that a mesh axis runs over, the one named last changes fastest.
Arguments:
- jacobian: bfloat16 [8192, 40960], P('obs', 'state'), may hold values from -0.125 to 0.125
- obs_weight: float32 [8192], P('obs'), may hold values from 0.25 to 4
- observed: float32 [8192], P('obs'), may hold values from -6 to 6
- prior_state: bfloat16 [40960], P('state'), may hold values from -1.1953125 to 1.1953125
- prior_std: bfloat16 [40960], P('state'), may hold values from 0.5 to 2
- owner_slot: int32 [40960], P('state'), may hold values from 0 to 40959, each once
Outputs:
- gram_band: float32 [32, 1280, 3, 1280], P('state', 'obs')
- gradient: float32 [40960], P('state')
Inputs may be any that keep to these rules, and one draw needn't show every extreme that they name: owner_slot names every position once.
All inputs are finite; a program needn't handle non-finite values.
Results may differ from a plain program's by a relative error of at most 0.0028.
Values may be sent and summed in bfloat16 or wider, within the bound.
No kernel may reach another device: no remote copies, remote signals or barrier semaphores. Data moves between devices by JAX's collectives and lax.ppermute only.
A program may use at most 128 MiB of HBM per device.

v0:
```python
import jax
import jax.numpy as jnp
from jax import lax
from jax.sharding import PartitionSpec as P


def shifted(value, axis, steps):
    count = lax.axis_size(axis)
    pairs = [(source, (source + steps) % count) for source in range(count)]
    return lax.ppermute(value, axis, pairs)


def cross_rows(left, right):
    return lax.dot_general(
        left, right, (((0,), (0,)), ((), ())), preferred_element_type=jnp.float32
    )


def on_device(jacobian, obs_weight, observed, prior_state, prior_std, owner_slot):
    width = jacobian.shape[1]
    quarter = width // lax.axis_size("obs")
    group = lax.axis_index("obs")
    weighted = (jacobian * obs_weight[:, None]).astype(jnp.bfloat16)
    spread = prior_std.astype(jnp.float32)
    rows_std = lax.dynamic_slice_in_dim(spread, group * quarter, quarter, 0)
    partial_model = jnp.dot(jacobian, prior_state, preferred_element_type=jnp.float32)
    model = lax.psum(partial_model, "state")
    misfit = (obs_weight * (observed - model)).astype(jnp.bfloat16)
    partial_descent = jnp.dot(misfit, jacobian, preferred_element_type=jnp.float32)
    descent = lax.psum(partial_descent, "obs")
    scaled = spread * descent
    next_cols, next_std = shifted((jacobian, prior_std), "state", -1)
    next_spread = next_std.astype(jnp.float32)
    far_cols, far_std = shifted((jacobian, prior_std), "state", -2)
    summed = lax.psum_scatter(
        jnp.concatenate(
            [
                cross_rows(weighted, jacobian),
                cross_rows(weighted, next_cols),
                cross_rows(weighted, far_cols),
            ],
            axis=1,
        ),
        "obs",
        scatter_dimension=0,
        tiled=True,
    )
    blocks = summed.reshape(quarter, 3, width)
    cols_std = jnp.stack([spread, next_spread, far_std.astype(jnp.float32)], axis=0)
    band = blocks * rows_std[:, None, None] * cols_std[None, :, :]
    dense = jnp.zeros((width * lax.axis_size("state"),), jnp.float32).at[owner_slot].set(scaled)
    gradient = lax.psum_scatter(dense, "state", scatter_dimension=0, tiled=True)
    return (band[None], gradient)


def solution(mesh):
    placed = (P("obs", "state"), P("obs"), P("obs"), P("state"), P("state"), P("state"))
    return jax.shard_map(
        on_device,
        mesh=mesh,
        in_specs=placed,
        out_specs=(P("state", "obs", None, None), P("state")),
        check_vma=False,
    )
```

profile of v0, /device:TPU:0, one launch (start us, length us, event | category | flops | bytes accessed | tf_op | source)
XLA Modules:
  0.0 732.0 jit_solution(15853517561895798853)
XLA Ops:
  8.0 0.0 copy-start.2
  8.0 0.0 copy-start.1
  8.0 0.0 all-reduce.3.cloned.1.call-start
  8.1 7.4 %collective-permute-start.1 = (bf16[2048,1280]{1,0:T(8,128)(2,1)}, bf16[2048,1280]{1,0:T(8,128)(2,1)}, u32[]{:S(2)}, u32[]{:S(2)}) collective-permute-start(bf16[2048,1280]{1,0:T(8,128)(2,1)} %param.6), channel_id=1, source_target_pairs={{0,30},{1,31},{2,0},{3,1},{4,2},{5,3},{6,4},{7,5},{8,6},{9,7},{10,... | collective-permute-start | bytes 15728648 | tf_op jit(solution)/shard_map/ppermute | solution.py:10
  15.5 0.7 collective-permute-start
  16.2 0.7 reshape.35
  16.9 0.0 copy-start.3
  16.9 0.0 copy-start
  16.9 4.0 fusion.8
  20.9 295.6 %psum.14 = f32[2048]{0:T(1024)S(1)} all-reduce(f32[2048]{0:T(1024)S(1)} %bitcast.14), channel_id=1, replica_groups=mesh['obs'=4,'state'=32] {'state'}, use_global_device_ids=true, to_apply=%region_1.0 | all-reduce | flops 2048 | bytes 16384 | tf_op jit(solution)/shard_map/psum | solution.py:27
  316.5 0.0 copy-done.2
  316.5 0.0 copy-done.1
  316.6 3.3 convolution_reduce_fusion
  319.9 7.3 psum.15
  327.1 0.0 copy-done.3
  327.2 0.0 copy-done
  327.2 5.9 scatter_custom_fusion
  333.1 0.0 all-reduce.3.cloned.1.call-update
  333.1 0.2 reduce-scatter.4.cloned.1.call-start
  333.3 0.0 slice-start
  333.3 11.0 %fusion.2 = f32[1280,1280]{0,1:T(8,128)S(1)} fusion(bf16[2048,1280]{1,0:T(8,128)(2,1)} %param.6, f32[2048]{0:T(1024)S(1)} %copy-done.2), kind=kOutput, calls=%fused_computation.5 | convolution fusion | flops 6718750720 | bytes 11804672 | tf_op jit(solution)/shard_map/dot_general | solution.py:14
  344.4 0.0 slice-start.1
  344.4 0.0 collective-permute-done.1
  344.4 11.0 %fusion = f32[1280,1280]{0,1:T(8,128)S(1)} fusion(bf16[2048,1280]{1,0:T(8,128)(2,1)} %collective-permute-done.1, bf16[2048,1280]{1,0:T(8,128)(2,1)} %param.6, f32[2048]{0:T(1024)S(1)} %copy-done.2), kind=kOutput, calls=%fused_computation.3 | convolution fusion | flops 6718750720 | bytes 17047552 | tf_op jit(solution)/shard_map/dot_general | solution.py:14
  355.4 0.0 collective-permute-done
  355.4 0.0 slice-done
  355.4 0.0 slice-done.1
  355.4 9.4 %fusion.1 = f32[1280,1280]{0,1:T(8,128)S(1)} fusion(bf16[2048,1280]{1,0:T(8,128)(2,1)} %collective-permute-done, bf16[2048,1280]{1,0:T(8,128)(2,1)S(1)} %bitcast.12, f32[2048]{0:T(1024)S(1)} %copy-done.2), kind=kOutput, calls=%fused_computation.4 | convolution fusion | flops 6718750720 | bytes 17047552 | tf_op jit(solution)/shard_map/dot_general | solution.py:14
  364.8 7.1 pad_maximum_fusion
  372.0 21.6 %copy.10 = f32[1280,3840]{1,0:T(8,128)} copy(f32[1280,3840]{0,1:T(8,128)} %pad_maximum_fusion) | data formatting | bytes 39321600
  393.5 0.0 copy-start.4
  393.5 0.0 reduce-scatter.4.cloned.1.call-update
  393.6 0.1 collective-permute-start.3
  393.6 0.1 collective-permute-start.2
  393.7 0.1 dynamic_slice.3
  393.8 0.4 copy-done.4
  394.2 0.6 dynamic-slice
  395.4 3.3 collective-permute-done.3
  398.7 0.0 collective-permute-done.2
  398.8 305.9 %all-reduce.3.cloned.1.call-done = f32[40960]{0:T(1024)} async-done(((f32[40960]{0:T(1024)}), f32[40960]{0:T(1024)}) %all-reduce.3.cloned.1.call-update) | async-done | bytes 163856
  704.7 1.4 dynamic-slice.1
  706.1 0.0 reduce-scatter.4.cloned.1.call-done
  706.1 6.1 copy.11
  712.2 7.3 copy.9
  719.4 5.2 multiply_multiply_fusion
  (9 shorter events, 0.1 us)
Async XLA Ops:
  8.0 308.5 %copy-start.2 = (f32[2048]{0:T(1024)S(1)}, f32[2048]{0:T(1024)}, u32[]{:S(2)}) copy-start(f32[2048]{0:T(1024)} %param.7) | copy-start | bytes 24580
  8.0 308.5 %copy-start.1 = (f32[2048]{0:T(1024)S(1)}, f32[2048]{0:T(1024)}, u32[]{:S(2)}) copy-start(f32[2048]{0:T(1024)} %param.8) | copy-start | bytes 24580
  8.0 696.7 %all-reduce.3.cloned.1.call-start = ((), (), s32[]{:S(2)}) async-start(), calls=%async_computation.2 | async-start | bytes 327680
  8.1 336.3 %collective-permute-start.1 = (bf16[2048,1280]{1,0:T(8,128)(2,1)}, bf16[2048,1280]{1,0:T(8,128)(2,1)}, u32[]{:S(2)}, u32[]{:S(2)}) collective-permute-start(bf16[2048,1280]{1,0:T(8,128)(2,1)} %param.6), channel_id=1, source_target_pairs={{0,30},{1,31},{2,0},{3,1},{4,2},{5,3},{6,4},{7,5},{8,6},{9,7},{10,... | collective-permute-start | bytes 15728648 | tf_op jit(solution)/shard_map/ppermute | solution.py:10
  15.5 339.9 %collective-permute-start = (bf16[2048,1280]{1,0:T(8,128)(2,1)}, bf16[2048,1280]{1,0:T(8,128)(2,1)}, u32[]{:S(2)}, u32[]{:S(2)}) collective-permute-start(bf16[2048,1280]{1,0:T(8,128)(2,1)} %param.6), channel_id=1, source_target_pairs={{0,31},{1,0},{2,1},{3,2},{4,3},{5,4},{6,5},{7,6},{8,7},{9,8},{10,9... | collective-permute-start | bytes 15728648 | tf_op jit(solution)/shard_map/ppermute | solution.py:10
  16.9 310.2 %copy-start.3 = (s32[1280]{0:T(1024)S(1)}, s32[1280]{0:T(1024)}, u32[]{:S(2)}) copy-start(s32[1280]{0:T(1024)} %param.11) | copy-start | bytes 15364
  16.9 310.3 %copy-start = (bf16[1280]{0:T(1024)(128)(2,1)S(1)}, bf16[1280]{0:T(1024)(128)(2,1)}, u32[]{:S(2)}) copy-start(bf16[1280]{0:T(1024)(128)(2,1)} %param.10) | copy-start | bytes 7684
  333.1 373.0 %reduce-scatter.4.cloned.1.call-start = ((), (), s32[]{:S(2)}) async-start(), calls=%async_computation.1 | async-start | bytes 24576000
  333.3 22.1 %slice-start = ((s8[5242880]{0:T(1024)(128)(4,1)}), s8[4194304]{0:T(1024)(128)(4,1)S(1)}, s32[]{:S(2)}) async-start(s8[5242880]{0:T(1024)(128)(4,1)} %bitcast.11), calls=%async_computation.3 | async-start | bytes 8388608
  344.4 11.0 %slice-start.1 = ((s8[5242880]{0:T(1024)(128)(4,1)}), s8[1048576]{0:T(1024)(128)(4,1)S(1)}, s32[]{:S(2)}) async-start(s8[5242880]{0:T(1024)(128)(4,1)} %bitcast.11), calls=%async_computation.4 | async-start | bytes 2097152
  393.5 0.7 copy-start.4
  393.6 5.2 collective-permute-start.3
  393.6 5.1 collective-permute-start.2
Sparse Core Ops, SparseCore 0:
  333.2 371.4 all-reduce.2
Sparse Core Ops, SparseCore 1:
  393.6 145.6 reduce-scatter.3
where the time goes:
time: 733 us; the launch traced here: 732 us
  waiting for transfers between devices  309 us (42%)
  blocking collectives  303 us (41%)
  local copies, waits for them, and re-layouts  44 us (6%)
  matrix products  38.6 us (5%)
  between operations  16.4 us (2%)
  other arithmetic  12.3 us (2%)
  starting transfers between devices  8.56 us (1%)
    unnamed x4, waiting for transfers between devices  306 us
    psum x1, blocking collectives, on_device(): model = lax.psum(partial_model, 'state')  296 us
    dot_general x3, matrix products, cross_rows(): lax.dot_general(left, right, (((0,), (0,)), ((), ())), preferred_element_...  31.4 us
    unnamed x19, local copies, waits for them, and re-layouts  30.7 us
  transfers between devices with their start and end apart: 6, of which 2 were waited for; matrix products, arithmetic and copies ran while one was open for 10% of the time, Pallas kernels for 0%

commit v1 on v0

v1 whole, which is shorter than its diff:
```python
import functools

import jax
import jax.numpy as jnp
from jax import lax
from jax.experimental import pallas as pl
from jax.experimental.pallas import tpu as pltpu
from jax.sharding import PartitionSpec as P


N_OBS, N_STATE = 4, 32
C, R = 1280, 2048
Q = C // N_OBS
HALF = C // 2
WIDE = 768
BF, F32 = jnp.bfloat16, jnp.float32


def over_state(value, target):
    return lax.ppermute(value, "state", [(s, target(s)) for s in range(N_STATE)])


def over_obs(value, flip):
    return lax.ppermute(value, "obs", [(o, o ^ flip) for o in range(N_OBS)])


def over_both(value, flip, target):
    pairs = [
        (o * N_STATE + s, (o ^ flip) * N_STATE + target(s))
        for o in range(N_OBS)
        for s in range(N_STATE)
    ]
    return lax.ppermute(value, ("obs", "state"), pairs)


def back(s):
    return (s - 1) % N_STATE


def along_z(k):
    return lambda s: s // 4 * 4 + (s + k) % 4


def along_x(s):
    return s ^ 4


def ring_y(s):
    return (s + 8 if s & 4 else s - 8) % N_STATE


def along_y(k):
    return lambda s: (s + 8 * k) % N_STATE


ROWS = 512


def prepare_kernel(picks, jac, weight, tall, cols, select, *, start):
    @pl.when(pl.program_id(0) == 0)
    def _():
        place = lax.broadcasted_iota(jnp.int32, (HALF, HALF), 0)
        source = lax.broadcasted_iota(jnp.int32, (HALF, HALF), 1)
        moved = jnp.where(picks[1] == 0, Q, 0)
        wanted = jnp.where(place < Q, place + moved, place - moved)
        select[...] = jnp.where(wanted == source, 1.0, 0.0).astype(BF)

    block = jac[...]
    cols[...] = block[:, start : start + cols.shape[1]]
    chosen = jnp.where(picks[0] == 0, block[:, :HALF], block[:, HALF:])
    turned = lax.dot_general(
        select[...], chosen, (((1,), (1,)), ((), ())), preferred_element_type=F32
    )
    tall[...] = (turned * weight[...]).astype(BF)


def prepare(jacobian, obs_weight, half, core, start, width):
    return pl.pallas_call(
        functools.partial(prepare_kernel, start=start),
        out_shape=(jax.ShapeDtypeStruct((HALF, R), BF), jax.ShapeDtypeStruct((R, width), BF)),
        grid_spec=pltpu.PrefetchScalarGridSpec(
            num_scalar_prefetch=1,
            grid=(R // ROWS,),
            in_specs=[
                pl.BlockSpec((ROWS, C), lambda i, q: (i, 0)),
                pl.BlockSpec((1, ROWS), lambda i, q: (0, i)),
            ],
            out_specs=(
                pl.BlockSpec((HALF, ROWS), lambda i, q: (0, i)),
                pl.BlockSpec((ROWS, width), lambda i, q: (i, 0)),
            ),
            scratch_shapes=[pltpu.VMEM((HALF, HALF), BF)],
        ),
    )(jnp.stack([half, core]), jacobian, obs_weight.reshape(1, R))


LINES = C // 128
PACKET = 24


def place_kernel(base, packets, out):
    hi_ids = lax.broadcasted_iota(jnp.int32, (16, C), 0)
    lo_ids = lax.broadcasted_iota(jnp.int32, (128, C), 0).astype(F32).astype(BF)
    one, zero = jnp.ones((128, C), BF), jnp.zeros((128, C), BF)

    def row(packet, first):
        return jnp.concatenate(
            [packet[first + k : first + k + 1, :] for k in range(LINES)], axis=1
        )

    def body(source, total):
        packet = packets[source]
        local = row(packet, 0).astype(jnp.int32) - base[0]
        value = row(packet, LINES)
        first = value.astype(BF).astype(F32)
        second = (value - first).astype(BF).astype(F32)
        third = value - first - second
        mine = (local >> 7) == hi_ids
        rows = jnp.concatenate(
            [jnp.where(mine, part, 0.0) for part in (first, second, third)], axis=0
        ).astype(BF)
        lane = (local & 127).astype(F32).astype(BF)
        spot = jnp.where(lane == lo_ids, one, zero)
        return total + lax.dot_general(
            rows, spot, (((1,), (1,)), ((), ())), preferred_element_type=F32
        )

    total = lax.fori_loop(0, N_STATE, body, jnp.zeros((48, 128), F32), unroll=4)
    total = total[:16] + total[16:32] + total[32:]
    for line in range(LINES):
        out[line * 128 : (line + 1) * 128] = total[line]


def place(base, packets):
    return pl.pallas_call(
        place_kernel,
        out_shape=jax.ShapeDtypeStruct((C,), F32),
        grid_spec=pltpu.PrefetchScalarGridSpec(
            num_scalar_prefetch=1,
            grid=(1,),
            in_specs=[pl.BlockSpec((N_STATE, PACKET, 128), lambda i, b: (0, 0, 0))],
            out_specs=pl.BlockSpec((C,), lambda i, b: (0,)),
        ),
        name="place",
    )(base.reshape(1), packets)


def same_kernel(source, out):
    out[...] = source[...]


def same(value):
    return pl.pallas_call(
        same_kernel, out_shape=jax.ShapeDtypeStruct(value.shape, value.dtype), name="same"
    )(value)


def dot(left, right):
    return jnp.dot(left, right, preferred_element_type=F32)


def whole(value):
    return pl.BlockSpec(value.shape, lambda i: (0,) * value.ndim)


def rows_of(shape):
    return pl.BlockSpec((Q, shape[1]), lambda i: (i, 0))


def pick(value, k):
    return pl.BlockSpec((Q, value.shape[1]), lambda i: (k, 0))


def product_kernel(first, second, right, out):
    @pl.when(pl.program_id(0) == 0)
    def _():
        out[...] = dot(first[...], right[...])

    @pl.when(pl.program_id(0) == 1)
    def _():
        out[...] = dot(second[...], right[...])


def product(first, second, right):
    shape = (HALF, right.shape[1])
    return pl.pallas_call(
        product_kernel,
        grid=(2,),
        out_shape=jax.ShapeDtypeStruct(shape, F32),
        in_specs=[pick(first, 0), pick(second, 0), whole(right)],
        out_specs=rows_of(shape),
    )(first, second, right)


def closing_kernel(first, second, right, got, part, own):
    @pl.when(pl.program_id(0) == 0)
    def _():
        part[...] = (dot(first[...], right[...]) + got[...]).astype(BF)

    @pl.when(pl.program_id(0) == 1)
    def _():
        own[...] = dot(second[...], right[...]) + got[...]


def closing(first, second, right, got):
    shapes = [jax.ShapeDtypeStruct((Q, right.shape[1]), dtype) for dtype in (BF, F32)]
    return pl.pallas_call(
        closing_kernel,
        grid=(2,),
        out_shape=tuple(shapes),
        in_specs=[pick(first, 1), pick(second, 1), whole(right), rows_of(got.shape)],
        out_specs=tuple(whole(shape) for shape in shapes),
    )(first, second, right, got)


def split_kernel(left, *refs):
    rights, (sent, kept) = refs[:-2], refs[-2:]
    start = 0
    for right in rights:
        cols = slice(start, start + right.shape[1])
        start = cols.stop
        value = dot(left[...], right[...])

        @pl.when(pl.program_id(0) == 0)
        def _():
            sent[:, cols] = value

        @pl.when(pl.program_id(0) == 1)
        def _():
            kept[:, cols] = value


def split_product(left, rights):
    shape = jax.ShapeDtypeStruct((Q, sum(right.shape[1] for right in rights)), F32)
    return pl.pallas_call(
        split_kernel,
        grid=(2,),
        out_shape=(shape,) * 2,
        in_specs=[rows_of(left.shape)] + [whole(right) for right in rights],
        out_specs=(whole(shape),) * 2,
    )(left, *rights)


SLAB_STEPS = 4


def band_kernel(own0, x0, own1, x1, own2, x2, near, far, both, rows, here, ahead, band):
    scale = rows[...]
    band[0] = (own0[...] + x0[...].astype(F32)) * scale * here[...]
    left = own1[...] + x1[...].astype(F32)
    right = own2[...] + x2[...].astype(F32)
    band[1] = jnp.concatenate([left, right], axis=1) * scale * ahead[...]
    total = jnp.concatenate([near[...], far[...]], axis=1).astype(F32)
    band[2] = (total + both[...].astype(F32)) * scale


def finish(parts, rows, here, ahead):
    size = Q // SLAB_STEPS
    specs = [pl.BlockSpec((size, p.shape[1]), lambda i: (i, 0)) for p in parts]
    line = pl.BlockSpec((1, C), lambda i: (0, 0))
    return pl.pallas_call(
        band_kernel,
        grid=(SLAB_STEPS,),
        out_shape=jax.ShapeDtypeStruct((3, Q, C), F32),
        in_specs=specs + [pl.BlockSpec((size, 1), lambda i: (i, 0)), line, line],
        out_specs=pl.BlockSpec((3, size, C), lambda i: (0, i, 0)),
        name="finish",
    )(*parts, rows[:, None], here[None, :], ahead[None, :])


REST = C - WIDE


def copies(sources, targets, sems, first):
    made = []
    for k, (source, target) in enumerate(zip(sources, targets)):
        made.append(pltpu.make_async_copy(source, target, sems.at[first + k]))
        made[-1].start()
    return made


def sent_both_kernel(po, n1, n2, b1, v_po, v1, v2, o1, sems):
    loads = copies([po.at[pl.ds(0, Q)], n2, n1], [v_po, v2, v1], sems, 0)
    for load in loads[:2]:
        load.wait()
    o1[:, WIDE:] = dot(v_po[...], v2[...])
    loads[2].wait()
    o1[:, :WIDE] = dot(v_po[...], v1[...])
    copies([o1], [b1], sems, 3)[0].wait()


def sent_rest_kernel(wp, wo, pp, n2, k2, b01, v_wp, v_wo, v_pp, v2, ok2, o01, sems):
    top = pl.ds(0, Q)
    sources = [n2, wp.at[top], wo.at[top], pp.at[top]]
    loads = copies(sources, [v2, v_wp, v_wo, v_pp], sems, 0)
    for load in loads[:2]:
        load.wait()
    ok2[:Q] = dot(v_wp[...], v2[...])
    loads[2].wait()
    ok2[Q:] = dot(v_wo[...], v2[...])
    stores = copies([ok2], [k2], sems, 4)
    loads[3].wait()
    o01[...] = dot(v_pp[...], v2[...])
    stores += copies([o01], [b01], sems, 5)
    for store in stores:
        store.wait()


def kept_both_kernel(po, n1, n2, got, scale, b1, v_po, v1, v2, o1, sems):
    loads = copies([po.at[pl.ds(Q, Q)], n2, n1], [v_po, v2, v1], sems, 0)
    for load in loads[:2]:
        load.wait()
    right = dot(v_po[...], v2[...]) + got[:, WIDE:]
    o1[:, WIDE:] = (right * scale[:, WIDE:]).astype(BF)
    loads[2].wait()
    left = dot(v_po[...], v1[...]) + got[:, :WIDE]
    o1[:, :WIDE] = (left * scale[:, :WIDE]).astype(BF)
    copies([o1], [b1], sems, 3)[0].wait()


def kept_rest_kernel(wp, pp, n2, g2, g01, scale, part, b01, *scratch):
    v_wp, v_pp, v2, o_part, o01, sems = scratch
    low = pl.ds(Q, Q)
    loads = copies([n2, wp.at[low], pp.at[low]], [v2, v_wp, v_pp], sems, 0)
    for load in loads[:2]:
        load.wait()
    o_part[...] = (dot(v_wp[...], v2[...]) + g2[:Q]).astype(BF)
    stores = copies([o_part], [part], sems, 3)
    loads[2].wait()
    far = dot(v_pp[...], v2[...]) + g01[...]
    o01[...] = (far * scale[:, WIDE:]).astype(BF)
    stores += copies([o01], [b01], sems, 4)
    for store in stores:
        store.wait()


def own_kernel(left, right, got, own):
    own[...] = dot(left[...], right[...]) + got[...]


def own_product(left, right, got):
    shape = jax.ShapeDtypeStruct((Q, right.shape[1]), F32)
    return pl.pallas_call(
        own_kernel,
        grid=(1,),
        out_shape=shape,
        in_specs=[pick(left, 1), whole(right), pick(got, 1)],
        out_specs=whole(shape),
    )(left, right, got)


def vmem(*shapes):
    return [pltpu.VMEM(shape, dtype) for shape, dtype in shapes]


ANYWHERE = pl.BlockSpec(memory_space=pl.ANY)
LEFT, NEAR, FAR = ((Q, R), BF), ((R, WIDE), BF), ((R, REST), BF)


def by_hand(kernel, operands, near, outs, loaded):
    shapes = [jax.ShapeDtypeStruct(*item) for item in outs]
    return pl.pallas_call(
        kernel,
        out_shape=tuple(shapes),
        in_specs=[ANYWHERE] * len(operands) + [pl.BlockSpec(memory_space=pltpu.VMEM)] * len(near),
        out_specs=(ANYWHERE,) * len(outs),
        scratch_shapes=vmem(*loaded, *outs)
        + [pltpu.SemaphoreType.DMA((len(loaded) + len(outs),))],
    )(*operands, *near)


def on_device(jacobian, obs_weight, observed, prior_state, prior_std, owner_slot):
    group = lax.axis_index("obs").astype(jnp.int32)
    block = lax.axis_index("state").astype(jnp.int32)
    half, core = group // 2, group % 2
    spread = prior_std.astype(F32)
    rows_std = lax.dynamic_slice_in_dim(spread, group * Q, Q, 0)

    next_std = over_state(prior_std, back).astype(F32)
    model = dot(jacobian, prior_state)
    wp, n1 = prepare(jacobian, obs_weight, 1 - half, core, 0, WIDE)
    model = model + sum(over_state(model, along_z(k)) for k in range(1, 4))
    model = model + over_state(model, along_x)
    model = model + sum(over_state(model, along_y(k)) for k in range(1, 4))
    misfit = (obs_weight * (observed - model)).astype(BF)
    descent = dot(misfit, jacobian)

    def packed(slots, values):
        parts = (slots.reshape(LINES, 128), values.reshape(LINES, 128))
        return jnp.concatenate(parts + (jnp.zeros((PACKET - 2 * LINES, 128), F32),))[None]

    descent = descent + over_obs(descent, 1)
    scaled = spread * descent
    slots = owner_slot.astype(F32)
    mine = jnp.concatenate([slots, scaled])
    other = over_both(mine, 0, lambda s: s ^ 4)
    scaled = scaled + over_both(scaled, 2, lambda s: s)
    other_scaled = other[C:] + over_both(mine[C:], 2, lambda s: s ^ 4)
    packet = jnp.concatenate([packed(slots, scaled), packed(other[:C], other_scaled)])

    packet, wp, n1 = lax.optimization_barrier((packet, wp, n1))
    next1 = over_state(n1, back)
    prev_p = over_state(wp, lambda s: (s + 1) % N_STATE)
    wo, n2 = prepare(jacobian, obs_weight, half, core, WIDE, C - WIDE)
    next2 = over_state(n2, back)
    prev_o = over_state(wo, lambda s: (s + 1) % N_STATE)
    packets = [packet]
    for _ in range(3):
        packets.append(over_state(packets[-1], ring_y))
    packet = same(jnp.concatenate(packets))
    packet = jnp.concatenate(
        [packet] + [over_state(packet, along_z(k)) for k in range(1, 4)]
    )
    gradient = place(block * C, packet)

    def exchanged(right):
        sent = product(wp, wo, right)
        got = over_obs(sent, 1)
        part, own = closing(wp, wo, right, got)
        return own, over_obs(part, 2)

    def returned(left, rights, flip, scales):
        sent, kept = split_product(left, rights)
        got = over_obs(sent, 1)
        part = ((kept + got) * scales[None, :]).astype(BF)
        return over_both(part, flip, back)

    own0, x0 = exchanged(jacobian)
    own1, x1 = exchanged(next1)
    spread = same(spread)
    rows_std = same(rows_std)
    b00 = returned(prev_p, [next1], 2, next_std[:WIDE])
    next_std = same(next_std)
    both = (prev_o, next1, next2)
    rest = (wp, wo, prev_p, next2)
    scale = next_std[None, :]
    (sent1,) = by_hand(sent_both_kernel, both, (), [((Q, C), F32)], [LEFT, NEAR, FAR])
    got1 = over_obs(sent1, 1)
    outs = [((HALF, REST), F32), ((Q, REST), F32)]
    sent2 = by_hand(sent_rest_kernel, rest, (), outs, [LEFT, LEFT, LEFT, FAR])
    got2 = [over_obs(value, 1) for value in sent2]
    outs = [((Q, C), BF)]
    (b1,) = by_hand(kept_both_kernel, both, (got1, scale), outs, [LEFT, NEAR, FAR])
    b1 = over_both(b1, 0, back)
    outs = [((Q, REST), BF)] * 2
    operands = (wp, prev_p, next2)
    part, b01 = by_hand(kept_rest_kernel, operands, (*got2, scale), outs, [LEFT, LEFT, FAR])
    x2 = over_obs(part, 2)
    b01 = over_both(b01, 2, back)

    own2 = own_product(wo, next2, got2[0])

    parts = (own0, x0, own1, x1, own2, x2, b00, b01, b1)
    band = finish(parts, rows_std, spread, next_std)
    return (jnp.transpose(band, (1, 0, 2))[None], gradient)


def solution(mesh):
    placed = (P("obs", "state"), P("obs"), P("obs"), P("state"), P("state"), P("state"))

    return jax.shard_map(
        on_device,
        mesh=mesh,
        in_specs=placed,
        out_specs=(P("state", "obs", None, None), P("state")),
        check_vma=False,
    )
```

time: 733 us -> 296 us (0.40)
  blocking collectives: 303 us -> 0 us
  waiting for transfers between devices: 309 us -> 108 us
  Pallas kernels: 0 us -> 96.3 us
  starting transfers between devices: 8.56 us -> 68.7 us
  local copies, waits for them, and re-layouts: 44 us -> 7.55 us
  matrix products: 38.6 us -> 7.24 us
  between operations: 16.4 us -> 0.89 us
    unnamed x4 -> x0, waiting for transfers between devices: 306 us -> none
    psum x2 -> x0, blocking collectives: 303 us -> none  [the longest x1 296 us: on_device(): model = lax.psum(partial_model, 'state')]
    ppermute x4 -> x34, waiting for transfers between devices: 3.33 us -> 108 us  [the longest x18 102 us: over_state(): lax.ppermute(value, 'state', [(s, target(s)) for s in range(N_STATE)])]
    pallas_call x0 -> x18, Pallas kernels: none -> 96.3 us  [the longest x4 24.4 us: by_hand(): pl.pallas_call(kernel, out_shape=tuple(shapes), in_specs=[ANYWHERE] * len...]
    ppermute x4 -> x34, starting transfers between devices: 8.3 us -> 68.7 us  [the longest x18 36.2 us: over_state(): lax.ppermute(value, 'state', [(s, target(s)) for s in range(N_STATE)])]
    dot_general x5 -> x2, matrix products: 38.6 us -> 7.24 us  [dot(): return jnp.dot(left, right, preferred_element_type=F32)]
    unnamed x19 -> x27, local copies, waits for them, and re-layouts: 30.7 us -> 2.79 us
  transfers between devices with their start and end apart: 6 -> 34, of which waited for: 2 -> 10; matrix products, arithmetic and copies ran while one was open for 10% -> 3% of each run, Pallas kernels for 0% -> 31%
where the time goes in v1:
time: 296 us; the launch traced here: 293 us
  waiting for transfers between devices  108 us (36%)
  Pallas kernels  96.3 us (33%)
  starting transfers between devices  68.7 us (23%)
  local copies, waits for them, and re-layouts  7.55 us (3%)
  matrix products  7.24 us (2%)
  other arithmetic  5.21 us (2%)
    ppermute x18, waiting for transfers between devices, over_state(): lax.ppermute(value, 'state', [(s, target(s)) for s in range(N_STATE)])  102 us
    ppermute x18, starting transfers between devices, over_state(): lax.ppermute(value, 'state', [(s, target(s)) for s in range(N_STATE)])  36.2 us
    ppermute x6, starting transfers between devices, over_both(): return lax.ppermute(value, ('obs', 'state'), pairs)  25.6 us
    pallas_call x4, Pallas kernels, by_hand(): pl.pallas_call(kernel, out_shape=tuple(shapes), in_specs=[ANYWHERE] * len...  24.4 us
    pallas_call x2, Pallas kernels, closing(): pl.pallas_call(closing_kernel, grid=(2,), out_shape=tuple(shapes), in_spe...  15.7 us
    pallas_call x2, Pallas kernels, prepare(): pl.pallas_call(functools.partial(prepare_kernel, start=start), out_shape=...  14.6 us
    pallas_call x2, Pallas kernels, product(): pl.pallas_call(product_kernel, grid=(2,), out_shape=jax.ShapeDtypeStruct(...  14.3 us
    dot_general x2, matrix products, dot(): return jnp.dot(left, right, preferred_element_type=F32)  7.24 us
  transfers between devices with their start and end apart: 34, of which 10 were waited for; matrix products, arithmetic and copies ran while one was open for 3% of the time, Pallas kernels for 31%

profile of v1, /device:TPU:0, one launch (start us, length us, event | category | flops | bytes accessed | tf_op | source)
XLA Modules:
  0.0 293.4 jit_solution(5351814145188027018)
XLA Ops:
  0.6 0.7 reshape.35
  1.3 4.0 %fusion.1 = f32[1,2048]{1,0:T(1,128)S(1)} fusion(bf16[2048,1280]{1,0:T(8,128)(2,1)} %right.3, bf16[1280,1]{0,1:T(2,128)(2,1)S(1)} %reshape.35), kind=kOutput, calls=%fused_computation.18 | convolution fusion | flops 5242880 | bytes 5253632 | tf_op jit(solution)/shard_map/dot_general | solution.py:159
  5.3 2.0 collective-permute-start
  7.3 3.6 %collective-permute-start.1 = (f32[2048]{0:T(1024)S(1)}, f32[2048]{0:T(1024)S(1)}, u32[]{:S(2)}, u32[]{:S(2)}) collective-permute-start(f32[2048]{0:T(1024)S(1)} %bitcast.29), channel_id=1, source_target_pairs={{0,2},{1,3},{2,0},{3,1},{4,6},{5,7},{6,4},{7,5},{8,10},{9,11},{10,... | collective-permute-start | bytes 24584 | tf_op jit(solution)/shard_map/ppermute | solution.py:20
  10.9 1.0 collective-permute-start.2
  11.9 0.7 collective-permute-done.1
  12.6 1.9 collective-permute-done.2
  14.6 1.5 collective-permute-start.3
  16.1 2.2 collective-permute-done.3
  18.2 1.6 collective-permute-start.4
  19.8 2.9 collective-permute-start.5
  22.7 1.3 collective-permute-start.6
  24.1 0.9 collective-permute-done.5
  25.0 1.4 collective-permute-done.6
  26.4 3.3 %convolution_reduce_fusion = f32[1280]{0:T(1024)S(1)} fusion(bf16[2048,1]{0,1:T(2,128)(2,1)S(1)} %reshape.37, bf16[2048,1280]{1,0:T(8,128)(2,1)} %right.3), kind=kOutput, calls=%fused_computation | convolution fusion | flops 5242880 | bytes 5252096 | tf_op jit(solution)/shard_map/dot_general | solution.py:159
  29.8 0.7 pad_add_fusion
  30.4 7.5 %shard_map.77 = (bf16[640,2048]{1,0:T(8,128)(2,1)}, bf16[2048,768]{1,0:T(8,128)(2,1)}) custom-call(s32[2]{0:T(128)} %get-tuple-element.42.picks, bf16[2048,1280]{1,0:T(8,128)(2,1)} %right.3, f32[1,2048]{1,0:T(1,128)} %bitcast.26), custom_call_target="tpu_custom_call" | custom-call | tf_op jit(solution)/shard_map/pallas_call | solution.py:78
  38.1 2.8 collective-permute-start.10
  40.9 0.8 collective-permute-start.8
  41.7 0.5 collective-permute-start.9
  42.2 3.8 %collective-permute-done.8 = f32[1280]{0:T(1024)S(1)} collective-permute-done((f32[1280]{0:T(1024)S(1)}, f32[1280]{0:T(1024)S(1)}, u32[]{:S(2)}, u32[]{:S(2)}) %collective-permute-start.8) | collective-permute-done | bytes 5152 | tf_op jit(solution)/shard_map/ppermute | solution.py:33
  46.2 3.9 %collective-permute-start.13 = (bf16[2048,768]{1,0:T(8,128)(2,1)}, bf16[2048,768]{1,0:T(8,128)(2,1)}, u32[]{:S(2)}, u32[]{:S(2)}) collective-permute-start(bf16[2048,768]{1,0:T(8,128)(2,1)} %get-tuple-element.25), channel_id=1, source_target_pairs={{0,31},{1,0},{2,1},{3,2},{4,3},{5,4},{6,5},{7,6},{8,7},{9,8},{10,9... | collective-permute-start | bytes 9437192 | tf_op jit(solution)/shard_map/ppermute | solution.py:20
  50.1 7.1 %shard_map.78 = (bf16[640,2048]{1,0:T(8,128)(2,1)}, bf16[2048,512]{1,0:T(8,128)(2,1)}) custom-call(s32[2]{0:T(128)} %get-tuple-element.43.picks, bf16[2048,1280]{1,0:T(8,128)(2,1)} %right.3, f32[1,2048]{1,0:T(1,128)} %bitcast.27), custom_call_target="tpu_custom_call" | custom-call | tf_op jit(solution)/shard_map/pallas_call | solution.py:78
  57.2 6.2 %collective-permute-start.16 = (bf16[2048,512]{1,0:T(8,128)(2,1)}, bf16[2048,512]{1,0:T(8,128)(2,1)}, u32[]{:S(2)}, u32[]{:S(2)}) collective-permute-start(bf16[2048,512]{1,0:T(8,128)(2,1)} %get-tuple-element.28), channel_id=1, source_target_pairs={{0,31},{1,0},{2,1},{3,2},{4,3},{5,4},{6,5},{7,6},{8,7},{9,8},{10,9... | collective-permute-start | bytes 6291464 | tf_op jit(solution)/shard_map/ppermute | solution.py:20
  63.4 8.2 %shard_map.79 = f32[640,1280]{1,0:T(8,128)} custom-call(bf16[640,2048]{1,0:T(8,128)(2,1)} %get-tuple-element.21.first.wp, bf16[640,2048]{1,0:T(8,128)(2,1)} %get-tuple-element.22.second.wo.left, bf16[2048,1280]{1,0:T(8,128)(2,1)} %right.3), custom_call_target="tpu_custom_call" | custom-call | tf_op jit(solution)/shard_map/pallas_call | solution.py:186
  71.6 90.3 %collective-permute-done.16.n2.right = bf16[2048,512]{1,0:T(8,128)(2,1)} collective-permute-done((bf16[2048,512]{1,0:T(8,128)(2,1)}, bf16[2048,512]{1,0:T(8,128)(2,1)}, u32[]{:S(2)}, u32[]{:S(2)}) %collective-permute-start.16) | collective-permute-done | bytes 2097184 | tf_op jit(solution)/shard_map/ppermute | solution.py:20
  161.9 6.0 %shard_map.87 = f32[320,1280]{1,0:T(8,128)} custom-call(bf16[640,2048]{1,0:T(8,128)(2,1)} %collective-permute-done.25.po, bf16[2048,768]{1,0:T(8,128)(2,1)} %collective-permute-done.13.right.refs_0_.n1, bf16[2048,512]{1,0:T(8,128)(2,1)} %collective-permute-done.16.n2.right), custom_call_target="tpu_custom_call" | custom-call | tf_op jit(solution)/shard_map/pallas_call | solution.py:362
  168.0 6.1 %shard_map.81 = f32[640,768]{1,0:T(8,128)} custom-call(bf16[640,2048]{1,0:T(8,128)(2,1)} %get-tuple-element.21.first.wp, bf16[640,2048]{1,0:T(8,128)(2,1)} %get-tuple-element.22.second.wo.left, bf16[2048,768]{1,0:T(8,128)(2,1)} %collective-permute-done.13.right.refs_0_.n1), custom_call_target="tpu_custom_call" | custom-call | tf_op jit(solution)/shard_map/pallas_call | solution.py:186
  174.5 1.2 collective-permute-start.28
  175.7 5.5 %collective-permute-start.20 = (bf16[1280]{0:T(1024)(128)(2,1)S(1)}, bf16[1280]{0:T(1024)(128)(2,1)S(1)}, u32[]{:S(2)}, u32[]{:S(2)}) collective-permute-start(bf16[1280]{0:T(1024)(128)(2,1)S(1)} %copy-done.10), channel_id=1, source_target_pairs={{0,31},{1,0},{2,1},{3,2},{4,3},{5,4},{6,5},{7,6},{8,7},{9,8},{10,9... | collective-permute-start | bytes 7688 | tf_op jit(solution)/shard_map/ppermute | solution.py:20
  181.2 6.0 %shard_map.86 = (f32[320,768]{1,0:T(8,128)}, f32[320,768]{1,0:T(8,128)}) custom-call(bf16[640,2048]{1,0:T(8,128)(2,1)} %collective-permute-done.17.pp.left, bf16[2048,768]{1,0:T(8,128)(2,1)} %collective-permute-done.13.right.refs_0_.n1), custom_call_target="tpu_custom_call" | custom-call | tf_op jit(solution)/shard_map/pallas_call | solution.py:235
  187.2 2.1 collective-permute-start.29
  189.3 1.8 collective-permute-done.29
  191.1 3.2 %collective-permute-start.30 = (f32[2,24,128]{2,1,0:T(8,128)S(1)}, f32[2,24,128]{2,1,0:T(8,128)S(1)}, u32[]{:S(2)}, u32[]{:S(2)}) collective-permute-start(f32[2,24,128]{2,1,0:T(8,128)S(1)} %collective-permute-done.29), channel_id=1, source_target_pairs={{0,24},{1,25},{2,26},{3,27},{4,12},{5,13},{6,14},{7,15},{8,0},{9,1... | collective-permute-start | bytes 73736 | tf_op jit(solution)/shard_map/ppermute | solution.py:20
  194.4 5.4 %shard_map.83 = (f32[640,512]{1,0:T(8,128)}, f32[320,512]{1,0:T(8,128)}) custom-call(bf16[640,2048]{1,0:T(8,128)(2,1)} %get-tuple-element.21.first.wp, bf16[640,2048]{1,0:T(8,128)(2,1)} %get-tuple-element.22.second.wo.left, bf16[640,2048]{1,0:T(8,128)(2,1)} %collective-permute-done.17.pp.left, bf16[2048,512]{1,0:T(8,128)(2,1)} %collective-permute-done.16.n2.right), custom_call_target="tpu_custom_call" | custom-call | tf_op jit(solution)/shard_map/pallas_call | solution.py:362
  199.8 0.6 pad_maximum_fusion.1.source
  200.5 1.5 same.7
  202.0 9.1 %shard_map.80 = (bf16[320,1280]{1,0:T(8,128)(2,1)}, f32[320,1280]{1,0:T(8,128)}) custom-call(bf16[640,2048]{1,0:T(8,128)(2,1)} %get-tuple-element.21.first.wp, bf16[640,2048]{1,0:T(8,128)(2,1)} %get-tuple-element.22.second.wo.left, bf16[2048,1280]{1,0:T(8,128)(2,1)} %right.3, f32[640,1280]{1,0:T(8,128)} %collective-permute-done.11.got), custom_call_target="tpu_custom_call" | custom-call | tf_op jit(solution)/shard_map/pallas_call | solution.py:207
  211.2 2.7 collective-permute-start.12
  214.0 0.6 convert_element_type.18.source
  214.6 1.3 same.4
  215.9 1.3 broadcast_in_dim.22.scale.ahead
  217.2 7.2 %shard_map.88 = bf16[320,1280]{1,0:T(8,128)(2,1)} custom-call(bf16[640,2048]{1,0:T(8,128)(2,1)} %collective-permute-done.25.po, bf16[2048,768]{1,0:T(8,128)(2,1)} %collective-permute-done.13.right.refs_0_.n1, bf16[2048,512]{1,0:T(8,128)(2,1)} %collective-permute-done.16.n2.right, f32[320,1280]{1,0:T(8,128)} %collective-permute-done.26.got, ...), custom_call_target="tpu_custom_call" | custom-call | tf_op jit(solution)/shard_map/pallas_call | solution.py:362
  224.4 2.0 collective-permute-start.27
  226.5 0.9 multiply_convert_fusion
  227.4 6.5 %shard_map.82 = (bf16[320,768]{1,0:T(8,128)(2,1)}, f32[320,768]{1,0:T(8,128)}) custom-call(bf16[640,2048]{1,0:T(8,128)(2,1)} %get-tuple-element.21.first.wp, bf16[640,2048]{1,0:T(8,128)(2,1)} %get-tuple-element.22.second.wo.left, bf16[2048,768]{1,0:T(8,128)(2,1)} %collective-permute-done.13.right.refs_0_.n1, f32[640,768]{1,0:T(8,128)} %collective-permute-done.14.got), custom_call_target="tpu_custom_call" | custom-call | tf_op jit(solution)/shard_map/pallas_call | solution.py:207
  233.9 19.3 %collective-permute-start.23 = (bf16[320,768]{1,0:T(8,128)(2,1)S(1)}, bf16[320,768]{1,0:T(8,128)(2,1)S(1)}, u32[]{:S(2)}, u32[]{:S(2)}) collective-permute-start(bf16[320,768]{1,0:T(8,128)(2,1)S(1)} %copy-done.3), channel_id=1, source_target_pairs={{0,95},{1,64},{2,65},{3,66},{4,67},{5,68},{6,69},{7,70},{8,71},{9,... | collective-permute-start | bytes 1474568 | tf_op jit(solution)/shard_map/ppermute | solution.py:33
  253.2 0.6 collective-permute-start.15
  253.8 1.0 copy-done.1
  254.9 5.9 %shard_map.85 = (bf16[320,512]{1,0:T(8,128)(2,1)}, bf16[320,512]{1,0:T(8,128)(2,1)}) custom-call(bf16[640,2048]{1,0:T(8,128)(2,1)} %get-tuple-element.21.first.wp, bf16[640,2048]{1,0:T(8,128)(2,1)} %collective-permute-done.17.pp.left, bf16[2048,512]{1,0:T(8,128)(2,1)} %collective-permute-done.16.n2.right, f32[640,512]{1,0:T(8,128)} %copy-done.1, ...), custom_call_target="tpu_custom_call" | custom-call | tf_op jit(solution)/shard_map/pallas_call | solution.py:362
  260.8 2.6 collective-permute-done.33
  263.4 2.7 collective-permute-start.21
  266.3 0.6 convert_element_type.16.source
  266.9 0.6 dynamic_slice.3.source
  267.5 1.3 same.5
  268.8 1.5 broadcast_in_dim.26.rows
  270.2 1.3 same.6
  271.5 1.3 broadcast_in_dim.24.here
  272.8 1.7 pad_maximum_fusion.packets
  274.5 6.2 %place.1 = f32[1280]{0:T(1024)} custom-call(s32[1]{0:T(128)} %bitcast.13.base, f32[32,24,128]{2,1,0:T(8,128)} %pad_maximum_fusion.packets), custom_call_target="tpu_custom_call" | custom-call | tf_op jit(solution)/shard_map/place/pallas_call | solution.py:135
  280.7 3.8 %shard_map.84.own2 = f32[320,512]{1,0:T(8,128)} custom-call(bf16[640,2048]{1,0:T(8,128)(2,1)} %get-tuple-element.22.second.wo.left, bf16[2048,512]{1,0:T(8,128)(2,1)} %collective-permute-done.16.n2.right, f32[640,512]{1,0:T(8,128)} %copy-done.1), custom_call_target="tpu_custom_call" | custom-call | tf_op jit(solution)/shard_map/pallas_call | solution.py:343
  284.5 2.0 collective-permute-done.24.far
  286.5 0.7 copy-done.8
  287.5 5.9 %finish.1 = f32[3,320,1280]{2,1,0:T(8,128)} custom-call(f32[320,1280]{1,0:T(8,128)} %get-tuple-element.23.own0, bf16[320,1280]{1,0:T(8,128)(2,1)} %collective-permute-done.12.x0, f32[320,768]{1,0:T(8,128)} %get-tuple-element.26.own1, bf16[320,768]{1,0:T(8,128)(2,1)} %copy-done.5, f32[320,512]{1,0:T(8,128)} %shard_map.84.own2, bf16[320,512]{1,0:T(8,128)(2,1)} %copy-done.7, ...), custom_call_target="tpu_custom_call" | custom-call | tf_op jit(solution)/shard_map/finish/pallas_call | solution.py:261
  (75 shorter events, 1.9 us)
Async XLA Ops:
  1.3 22.7 %copy-start.11 = (s32[1280]{0:T(1024)S(1)}, s32[1280]{0:T(1024)}, u32[]{:S(2)}) copy-start(s32[1280]{0:T(1024)} %param.11) | copy-start | bytes 15364
  1.3 25.1 %copy-start.9 = (f32[2048]{0:T(1024)S(1)}, f32[2048]{0:T(1024)}, u32[]{:S(2)}) copy-start(f32[2048]{0:T(1024)} %param.7) | copy-start | bytes 24580
  1.3 25.0 %copy-start.12 = (f32[2048]{0:T(1024)S(1)}, f32[2048]{0:T(1024)}, u32[]{:S(2)}) copy-start(f32[2048]{0:T(1024)} %param.8) | copy-start | bytes 24580
  5.3 6.6 %collective-permute-start = (f32[2048]{0:T(1024)S(1)}, f32[2048]{0:T(1024)S(1)}, u32[]{:S(2)}, u32[]{:S(2)}) collective-permute-start(f32[2048]{0:T(1024)S(1)} %bitcast.28), channel_id=1, source_target_pairs={{0,1},{1,2},{2,3},{3,0},{4,5},{5,6},{6,7},{7,4},{8,9},{9,10},{10,1... | collective-permute-start | bytes 24584 | tf_op jit(solution)/shard_map/ppermute | solution.py:20
  7.3 5.3 %collective-permute-start.1 = (f32[2048]{0:T(1024)S(1)}, f32[2048]{0:T(1024)S(1)}, u32[]{:S(2)}, u32[]{:S(2)}) collective-permute-start(f32[2048]{0:T(1024)S(1)} %bitcast.29), channel_id=1, source_target_pairs={{0,2},{1,3},{2,0},{3,1},{4,6},{5,7},{6,4},{7,5},{8,10},{9,11},{10,... | collective-permute-start | bytes 24584 | tf_op jit(solution)/shard_map/ppermute | solution.py:20
  10.9 3.7 %collective-permute-start.2 = (f32[2048]{0:T(1024)S(1)}, f32[2048]{0:T(1024)S(1)}, u32[]{:S(2)}, u32[]{:S(2)}) collective-permute-start(f32[2048]{0:T(1024)S(1)} %bitcast.30), channel_id=1, source_target_pairs={{0,3},{1,0},{2,1},{3,2},{4,7},{5,4},{6,5},{7,6},{8,11},{9,8},{10,9... | collective-permute-start | bytes 24584 | tf_op jit(solution)/shard_map/ppermute | solution.py:20
  14.6 3.7 %collective-permute-start.3 = (f32[2048]{0:T(1024)S(1)}, f32[2048]{0:T(1024)S(1)}, u32[]{:S(2)}, u32[]{:S(2)}) collective-permute-start(f32[2048]{0:T(1024)S(1)} %add_add_fusion), channel_id=1, source_target_pairs={{0,4},{1,5},{2,6},{3,7},{4,0},{5,1},{6,2},{7,3},{8,12},{9,13},{10,... | collective-permute-start | bytes 24584 | tf_op jit(solution)/shard_map/ppermute | solution.py:20
  18.2 5.8 %collective-permute-start.4 = (f32[2048]{0:T(1024)S(1)}, f32[2048]{0:T(1024)S(1)}, u32[]{:S(2)}, u32[]{:S(2)}) collective-permute-start(f32[2048]{0:T(1024)S(1)} %add.44), channel_id=1, source_target_pairs={{0,8},{1,9},{2,10},{3,11},{4,12},{5,13},{6,14},{7,15},{8,16},{9,17... | collective-permute-start | bytes 24584 | tf_op jit(solution)/shard_map/ppermute | solution.py:20
  19.8 5.2 %collective-permute-start.5 = (f32[2048]{0:T(1024)S(1)}, f32[2048]{0:T(1024)S(1)}, u32[]{:S(2)}, u32[]{:S(2)}) collective-permute-start(f32[2048]{0:T(1024)S(1)} %add.44), channel_id=1, source_target_pairs={{0,16},{1,17},{2,18},{3,19},{4,20},{5,21},{6,22},{7,23},{8,24},{9,... | collective-permute-start | bytes 24584 | tf_op jit(solution)/shard_map/ppermute | solution.py:20
  22.7 3.7 %collective-permute-start.6 = (f32[2048]{0:T(1024)S(1)}, f32[2048]{0:T(1024)S(1)}, u32[]{:S(2)}, u32[]{:S(2)}) collective-permute-start(f32[2048]{0:T(1024)S(1)} %add.44), channel_id=1, source_target_pairs={{0,24},{1,25},{2,26},{3,27},{4,28},{5,29},{6,30},{7,31},{8,0},{9,1... | collective-permute-start | bytes 24584 | tf_op jit(solution)/shard_map/ppermute | solution.py:20
  29.7 8.4 %collective-permute-start.7 = (f32[1280]{0:T(1024)S(1)}, f32[1280]{0:T(1024)S(1)}, u32[]{:S(2)}, u32[]{:S(2)}) collective-permute-start(f32[1280]{0:T(1024)S(1)} %convolution_reduce_fusion), channel_id=1, source_target_pairs={{0,32},{32,0},{64,96},{96,64},{1,33},{33,1},{65,97},{97,65},{2,34}... | collective-permute-start | bytes 15368 | tf_op jit(solution)/shard_map/ppermute | solution.py:24
  30.4 7.6 %copy-start.10 = (bf16[1280]{0:T(1024)(128)(2,1)S(1)}, bf16[1280]{0:T(1024)(128)(2,1)}, u32[]{:S(2)}) copy-start(bf16[1280]{0:T(1024)(128)(2,1)} %param.10) | copy-start | bytes 7684
  38.1 8.0 %collective-permute-start.10 = (f32[1280]{0:T(1024)S(1)}, f32[1280]{0:T(1024)S(1)}, u32[]{:S(2)}, u32[]{:S(2)}) collective-permute-start(f32[1280]{0:T(1024)S(1)} %add_multiply_fusion), channel_id=1, source_target_pairs={{0,68},{1,69},{2,70},{3,71},{4,64},{5,65},{6,66},{7,67},{8,76},{9,... | collective-permute-start | bytes 15368 | tf_op jit(solution)/shard_map/ppermute | solution.py:33
  40.9 5.2 %collective-permute-start.8 = (f32[1280]{0:T(1024)S(1)}, f32[1280]{0:T(1024)S(1)}, u32[]{:S(2)}, u32[]{:S(2)}) collective-permute-start(f32[1280]{0:T(1024)S(1)} %add_multiply_fusion), channel_id=1, source_target_pairs={{0,64},{1,65},{2,66},{3,67},{4,68},{5,69},{6,70},{7,71},{8,72},{9,... | collective-permute-start | bytes 15368 | tf_op jit(solution)/shard_map/ppermute | solution.py:33
  41.7 4.4 %collective-permute-start.9 = (f32[2560]{0:T(1024)S(1)}, f32[2560]{0:T(1024)S(1)}, u32[]{:S(2)}, u32[]{:S(2)}) collective-permute-start(f32[2560]{0:T(1024)S(1)} %pad_maximum_fusion.3), channel_id=1, source_target_pairs={{0,4},{1,5},{2,6},{3,7},{4,0},{5,1},{6,2},{7,3},{8,12},{9,13},{10,... | collective-permute-start | bytes 30728 | tf_op jit(solution)/shard_map/ppermute | solution.py:33
  46.2 115.7 %collective-permute-start.13 = (bf16[2048,768]{1,0:T(8,128)(2,1)}, bf16[2048,768]{1,0:T(8,128)(2,1)}, u32[]{:S(2)}, u32[]{:S(2)}) collective-permute-start(bf16[2048,768]{1,0:T(8,128)(2,1)} %get-tuple-element.25), channel_id=1, source_target_pairs={{0,31},{1,0},{2,1},{3,2},{4,3},{5,4},{6,5},{7,6},{8,7},{9,8},{10,9... | collective-permute-start | bytes 9437192 | tf_op jit(solution)/shard_map/ppermute | solution.py:20
  57.2 104.7 %collective-permute-start.25 = (bf16[640,2048]{1,0:T(8,128)(2,1)}, bf16[640,2048]{1,0:T(8,128)(2,1)}, u32[]{:S(2)}, u32[]{:S(2)}) collective-permute-start(bf16[640,2048]{1,0:T(8,128)(2,1)} %get-tuple-element.22.second.wo.left), channel_id=1, source_target_pairs={{0,1},{1,2},{2,3},{3,4},{4,5},{5,6},{6,7},{7,8},{8,9},{9,10},{10,1... | collective-permute-start | bytes 7864328 | tf_op jit(solution)/shard_map/ppermute | solution.py:20
  57.2 14.4 %copy-start = (bf16[640,2048]{1,0:T(8,128)(2,1)S(1)}, bf16[640,2048]{1,0:T(8,128)(2,1)}, u32[]{:S(2)}) copy-start(bf16[640,2048]{1,0:T(8,128)(2,1)} %get-tuple-element.21.first.wp) | copy-start | bytes 7864324
  57.2 104.7 %collective-permute-start.16 = (bf16[2048,512]{1,0:T(8,128)(2,1)}, bf16[2048,512]{1,0:T(8,128)(2,1)}, u32[]{:S(2)}, u32[]{:S(2)}) collective-permute-start(bf16[2048,512]{1,0:T(8,128)(2,1)} %get-tuple-element.28), channel_id=1, source_target_pairs={{0,31},{1,0},{2,1},{3,2},{4,3},{5,4},{6,5},{7,6},{8,7},{9,8},{10,9... | collective-permute-start | bytes 6291464 | tf_op jit(solution)/shard_map/ppermute | solution.py:20
  71.6 130.4 %collective-permute-start.11 = (f32[640,1280]{1,0:T(8,128)}, f32[640,1280]{1,0:T(8,128)}, u32[]{:S(2)}, u32[]{:S(2)}) collective-permute-start(f32[640,1280]{1,0:T(8,128)} %shard_map.79), channel_id=1, source_target_pairs={{0,32},{32,0},{64,96},{96,64},{1,33},{33,1},{65,97},{97,65},{2,34}... | collective-permute-start | bytes 9830408 | tf_op jit(solution)/shard_map/ppermute | solution.py:24
  71.6 104.0 %collective-permute-start.17 = (bf16[640,2048]{1,0:T(8,128)(2,1)S(1)}, bf16[640,2048]{1,0:T(8,128)(2,1)}, u32[]{:S(2)}, u32[]{:S(2)}) collective-permute-start(bf16[640,2048]{1,0:T(8,128)(2,1)S(1)} %copy-done), channel_id=1, source_target_pairs={{0,1},{1,2},{2,3},{3,4},{4,5},{5,6},{6,7},{7,8},{8,9},{9,10},{10,1... | collective-permute-start | bytes 7864328 | tf_op jit(solution)/shard_map/ppermute | solution.py:20
  167.9 46.0 %collective-permute-start.26 = (f32[320,1280]{1,0:T(8,128)}, f32[320,1280]{1,0:T(8,128)}, u32[]{:S(2)}, u32[]{:S(2)}) collective-permute-start(f32[320,1280]{1,0:T(8,128)} %shard_map.87), channel_id=1, source_target_pairs={{0,32},{32,0},{64,96},{96,64},{1,33},{33,1},{65,97},{97,65},{2,34}... | collective-permute-start | bytes 4915208 | tf_op jit(solution)/shard_map/ppermute | solution.py:24
  174.0 52.4 %collective-permute-start.14 = (f32[640,768]{1,0:T(8,128)}, f32[640,768]{1,0:T(8,128)}, u32[]{:S(2)}, u32[]{:S(2)}) collective-permute-start(f32[640,768]{1,0:T(8,128)} %shard_map.81), channel_id=1, source_target_pairs={{0,32},{32,0},{64,96},{96,64},{1,33},{33,1},{65,97},{97,65},{2,34}... | collective-permute-start | bytes 5898248 | tf_op jit(solution)/shard_map/ppermute | solution.py:24
  174.5 12.8 %collective-permute-start.28 = (f32[2,24,128]{2,1,0:T(8,128)S(1)}, f32[2,24,128]{2,1,0:T(8,128)S(1)}, u32[]{:S(2)}, u32[]{:S(2)}) collective-permute-start(f32[2,24,128]{2,1,0:T(8,128)S(1)} %pad_maximum_fusion.2), channel_id=1, source_target_pairs={{0,24},{1,25},{2,26},{3,27},{4,12},{5,13},{6,14},{7,15},{8,0},{9,1... | collective-permute-start | bytes 73736 | tf_op jit(solution)/shard_map/ppermute | solution.py:20
  175.7 11.6 %collective-permute-start.20 = (bf16[1280]{0:T(1024)(128)(2,1)S(1)}, bf16[1280]{0:T(1024)(128)(2,1)S(1)}, u32[]{:S(2)}, u32[]{:S(2)}) collective-permute-start(bf16[1280]{0:T(1024)(128)(2,1)S(1)} %copy-done.10), channel_id=1, source_target_pairs={{0,31},{1,0},{2,1},{3,2},{4,3},{5,4},{6,5},{7,6},{8,7},{9,8},{10,9... | collective-permute-start | bytes 7688 | tf_op jit(solution)/shard_map/ppermute | solution.py:20
  187.2 37.2 %collective-permute-start.22 = (f32[320,768]{1,0:T(8,128)}, f32[320,768]{1,0:T(8,128)S(1)}, u32[]{:S(2)}, u32[]{:S(2)}) collective-permute-start(f32[320,768]{1,0:T(8,128)} %get-tuple-element.33), channel_id=1, source_target_pairs={{0,32},{32,0},{64,96},{96,64},{1,33},{33,1},{65,97},{97,65},{2,34}... | collective-permute-start | bytes 2949128 | tf_op jit(solution)/shard_map/ppermute | solution.py:24
  187.2 3.9 %collective-permute-start.29 = (f32[2,24,128]{2,1,0:T(8,128)S(1)}, f32[2,24,128]{2,1,0:T(8,128)S(1)}, u32[]{:S(2)}, u32[]{:S(2)}) collective-permute-start(f32[2,24,128]{2,1,0:T(8,128)S(1)} %collective-permute-done.28), channel_id=1, source_target_pairs={{0,24},{1,25},{2,26},{3,27},{4,12},{5,13},{6,14},{7,15},{8,0},{9,1... | collective-permute-start | bytes 73736 | tf_op jit(solution)/shard_map/ppermute | solution.py:20
  191.1 8.6 %collective-permute-start.30 = (f32[2,24,128]{2,1,0:T(8,128)S(1)}, f32[2,24,128]{2,1,0:T(8,128)S(1)}, u32[]{:S(2)}, u32[]{:S(2)}) collective-permute-start(f32[2,24,128]{2,1,0:T(8,128)S(1)} %collective-permute-done.29), channel_id=1, source_target_pairs={{0,24},{1,25},{2,26},{3,27},{4,12},{5,13},{6,14},{7,15},{8,0},{9,1... | collective-permute-start | bytes 73736 | tf_op jit(solution)/shard_map/ppermute | solution.py:20
  199.8 54.1 %collective-permute-start.18 = (f32[640,512]{1,0:T(8,128)}, f32[640,512]{1,0:T(8,128)S(1)}, u32[]{:S(2)}, u32[]{:S(2)}) collective-permute-start(f32[640,512]{1,0:T(8,128)} %get-tuple-element.29), channel_id=1, source_target_pairs={{0,32},{32,0},{64,96},{96,64},{1,33},{33,1},{65,97},{97,65},{2,34}... | collective-permute-start | bytes 3932168 | tf_op jit(solution)/shard_map/ppermute | solution.py:24
  202.0 9.1 %collective-permute-start.31 = (f32[8,24,128]{2,1,0:T(8,128)}, f32[8,24,128]{2,1,0:T(8,128)S(1)}, u32[]{:S(2)}, u32[]{:S(2)}) collective-permute-start(f32[8,24,128]{2,1,0:T(8,128)} %same.7), channel_id=1, source_target_pairs={{0,1},{1,2},{2,3},{3,0},{4,5},{5,6},{6,7},{7,4},{8,9},{9,10},{10,1... | collective-permute-start | bytes 294920 | tf_op jit(solution)/shard_map/ppermute | solution.py:20
  211.2 54.9 %collective-permute-start.12 = (bf16[320,1280]{1,0:T(8,128)(2,1)}, bf16[320,1280]{1,0:T(8,128)(2,1)}, u32[]{:S(2)}, u32[]{:S(2)}) collective-permute-start(bf16[320,1280]{1,0:T(8,128)(2,1)} %get-tuple-element.24), channel_id=1, source_target_pairs={{0,64},{32,96},{64,0},{96,32},{1,65},{33,97},{65,1},{97,33},{2,66}... | collective-permute-start | bytes 2457608 | tf_op jit(solution)/shard_map/ppermute | solution.py:24
  213.8 39.4 %collective-permute-start.19 = (f32[320,512]{1,0:T(8,128)}, f32[320,512]{1,0:T(8,128)}, u32[]{:S(2)}, u32[]{:S(2)}) collective-permute-start(f32[320,512]{1,0:T(8,128)} %get-tuple-element.30), channel_id=1, source_target_pairs={{0,32},{32,0},{64,96},{96,64},{1,33},{33,1},{65,97},{97,65},{2,34}... | collective-permute-start | bytes 1966088 | tf_op jit(solution)/shard_map/ppermute | solution.py:24
  217.2 9.2 %copy-start.6 = (f32[8,24,128]{2,1,0:T(8,128)S(1)}, f32[8,24,128]{2,1,0:T(8,128)}, u32[]{:S(2)}) copy-start(f32[8,24,128]{2,1,0:T(8,128)} %same.7) | copy-start | bytes 294916
  217.2 9.3 %copy-start.2 = (f32[320,768]{1,0:T(8,128)S(1)}, f32[320,768]{1,0:T(8,128)}, u32[]{:S(2)}) copy-start(f32[320,768]{1,0:T(8,128)} %get-tuple-element.32) | copy-start | bytes 2949124
  224.4 62.1 %collective-permute-start.27 = (bf16[320,1280]{1,0:T(8,128)(2,1)}, bf16[320,1280]{1,0:T(8,128)(2,1)}, u32[]{:S(2)}, u32[]{:S(2)}) collective-permute-start(bf16[320,1280]{1,0:T(8,128)(2,1)} %shard_map.88), channel_id=1, source_target_pairs={{0,31},{1,0},{2,1},{3,2},{4,3},{5,4},{6,5},{7,6},{8,7},{9,8},{10,9... | collective-permute-start | bytes 2457608 | tf_op jit(solution)/shard_map/ppermute | solution.py:33
  226.4 7.6 %collective-permute-start.32 = (f32[8,24,128]{2,1,0:T(8,128)S(1)}, f32[8,24,128]{2,1,0:T(8,128)}, u32[]{:S(2)}, u32[]{:S(2)}) collective-permute-start(f32[8,24,128]{2,1,0:T(8,128)S(1)} %copy-done.6), channel_id=1, source_target_pairs={{0,2},{1,3},{2,0},{3,1},{4,6},{5,7},{6,4},{7,5},{8,10},{9,11},{10,... | collective-permute-start | bytes 294920 | tf_op jit(solution)/shard_map/ppermute | solution.py:20
  227.4 6.6 %copy-start.3 = (bf16[320,768]{1,0:T(8,128)(2,1)S(1)}, bf16[320,768]{1,0:T(8,128)(2,1)}, u32[]{:S(2)}) copy-start(bf16[320,768]{1,0:T(8,128)(2,1)} %multiply_convert_fusion) | copy-start | bytes 1474564
  233.9 52.5 %collective-permute-start.23 = (bf16[320,768]{1,0:T(8,128)(2,1)S(1)}, bf16[320,768]{1,0:T(8,128)(2,1)S(1)}, u32[]{:S(2)}, u32[]{:S(2)}) collective-permute-start(bf16[320,768]{1,0:T(8,128)(2,1)S(1)} %copy-done.3), channel_id=1, source_target_pairs={{0,95},{1,64},{2,65},{3,66},{4,67},{5,68},{6,69},{7,70},{8,71},{9,... | collective-permute-start | bytes 1474568 | tf_op jit(solution)/shard_map/ppermute | solution.py:33
  253.2 33.3 %collective-permute-start.15 = (bf16[320,768]{1,0:T(8,128)(2,1)}, bf16[320,768]{1,0:T(8,128)(2,1)S(1)}, u32[]{:S(2)}, u32[]{:S(2)}) collective-permute-start(bf16[320,768]{1,0:T(8,128)(2,1)} %get-tuple-element.27), channel_id=1, source_target_pairs={{0,64},{32,96},{64,0},{96,32},{1,65},{33,97},{65,1},{97,33},{2,66}... | collective-permute-start | bytes 1474568 | tf_op jit(solution)/shard_map/ppermute | solution.py:24
  253.8 1.1 copy-start.1
  253.8 9.6 %collective-permute-start.33 = (f32[8,24,128]{2,1,0:T(8,128)S(1)}, f32[8,24,128]{2,1,0:T(8,128)S(1)}, u32[]{:S(2)}, u32[]{:S(2)}) collective-permute-start(f32[8,24,128]{2,1,0:T(8,128)S(1)} %copy-done.6), channel_id=1, source_target_pairs={{0,3},{1,0},{2,1},{3,2},{4,7},{5,4},{6,5},{7,6},{8,11},{9,8},{10,9... | collective-permute-start | bytes 294920 | tf_op jit(solution)/shard_map/ppermute | solution.py:20
  263.4 21.1 %collective-permute-start.21 = (bf16[320,512]{1,0:T(8,128)(2,1)}, bf16[320,512]{1,0:T(8,128)(2,1)S(1)}, u32[]{:S(2)}, u32[]{:S(2)}) collective-permute-start(bf16[320,512]{1,0:T(8,128)(2,1)} %get-tuple-element.31), channel_id=1, source_target_pairs={{0,64},{32,96},{64,0},{96,32},{1,65},{33,97},{65,1},{97,33},{2,66}... | collective-permute-start | bytes 983048 | tf_op jit(solution)/shard_map/ppermute | solution.py:24
  266.1 20.4 %collective-permute-start.24 = (bf16[320,512]{1,0:T(8,128)(2,1)}, bf16[320,512]{1,0:T(8,128)(2,1)S(1)}, u32[]{:S(2)}, u32[]{:S(2)}) collective-permute-start(bf16[320,512]{1,0:T(8,128)(2,1)} %get-tuple-element.34), channel_id=1, source_target_pairs={{0,95},{1,64},{2,65},{3,66},{4,67},{5,68},{6,69},{7,70},{8,71},{9,... | collective-permute-start | bytes 983048 | tf_op jit(solution)/shard_map/ppermute | solution.py:33
  284.5 2.0 copy-start.7
  286.4 0.7 copy-start.8
  286.5 0.9 copy-start.4
  286.5 1.0 copy-start.5
